TPU v7x, 32 devices: a whole 2x2x4 slice. The times are simulated.
32 devices in a mesh: dp: 8 (over z, x), tensor: 4 (over y, core).
Axes of the slice: x: 2, y: 2, z: 4, core: 2. Of those that a mesh axis runs over, the one named last changes fastest.
Arguments:
- segments: bfloat16 [32, 704, 512], P('dp'), may hold values from -6 to 6
- seg_start: int32 [32, 704], P('dp'), may hold values from 0 to 2048, as said below
- seg_count: int32 [32], P('dp'), may hold values from 300 to 704, as said below
- norm_gain: bfloat16 [512], P('dp'), may hold values from 0.25 to 1.75
- norm_shift: bfloat16 [512], P('dp'), may hold values from -3 to 3
- qkv_weight: bfloat16 [512, 3, 512], P('dp', None, 'tensor'), may hold values from -0.25 to 0.25
- out_weight: bfloat16 [512, 512], P(('tensor', 'dp')), may hold values from -1 to 1
- ffn_gain: bfloat16 [512], P('dp'), may hold values from 0.25 to 1.75
- ffn_shift: bfloat16 [512], P('dp'), may hold values from -3 to 3
- up_weight: bfloat16 [512, 2048], P('dp', 'tensor'), may hold values from -0.25 to 0.25
- up_bias: bfloat16 [2048], P(('tensor', 'dp')), may hold values from -3 to 3
- down_weight: bfloat16 [2048, 512], P(('tensor', 'dp')), may hold values from -0.125 to 0.125
- cotangent: bfloat16 [32, 704, 512], P('dp'), may hold values from -6 to 6
Outputs:
- block_out: bfloat16 [32, 704, 512], P('dp')
- segments_grad: float32 [32, 704, 512], P('dp')
- norm_gain_grad: float32 [512], P('dp')
- norm_shift_grad: float32 [512], P('dp')
- qkv_weight_grad: float32 [512, 3, 512], P('dp', None, 'tensor')
- out_weight_grad: float32 [512, 512], P(('tensor', 'dp'))
- ffn_gain_grad: float32 [512], P('dp')
- ffn_shift_grad: float32 [512], P('dp')
- up_weight_grad: float32 [512, 2048], P('dp', 'tensor')
- up_bias_grad: float32 [2048], P(('tensor', 'dp'))
- down_weight_grad: float32 [2048, 512], P(('tensor', 'dp'))
Inputs may be any that keep to these rules, and one draw needn't show every extreme that they name: One sequence has exactly 704 live segments and one exactly 300; slots at and after seg_count are padding. `seg_start`: 0 in the first slot, strictly rising over a sequence's live segments and below 2048 there; 2048 in every padded slot.
All inputs are finite; a program needn't handle non-finite values.
Results may differ from a plain program's by a relative error of at most 0.014.
Values may be sent and summed in bfloat16 or wider, within the bound.
No kernel may reach another device: no remote copies, remote signals or barrier semaphores. Data moves between devices by JAX's collectives and lax.ppermute only.
A program may use at most 128 MiB of HBM per device.

v0:
```python
import math
import jax
import jax.numpy as jnp
from jax import lax
from jax.sharding import PartitionSpec as P

HEAD = 64
EPSILON = 1e-05
MASKED = -1e30


def split_up(array, dim, devices):
    dims = array.shape
    pieces = array.reshape(*dims[:dim], devices, dims[dim] // devices, *dims[dim + 1 :])
    return jnp.moveaxis(pieces, dim, 0)


def summed_on_arrival(array, axis, dim):
    pieces = split_up(array, dim, lax.axis_size(axis))
    arrived = lax.all_to_all(pieces, axis, split_axis=0, concat_axis=0, tiled=True)
    return arrived.astype(jnp.float32).sum(axis=0)


def sent_together(arrays, axis, dim, along):
    widths = [math.prod(a.shape[along:]) for a in arrays]
    both = jnp.concatenate(
        [a.reshape(*a.shape[:along], w) for a, w in zip(arrays, widths)], axis=along
    )
    filled = summed_on_arrival(both, axis, dim)
    pieces = jnp.split(filled, [sum(widths[:k]) for k in range(1, len(widths))], axis=along)
    return tuple(
        (b.reshape(*filled.shape[:along], *a.shape[along:]) for a, b in zip(arrays, pieces))
    )


def normalize(values, scale_vec, offset_vec):
    centre = jnp.mean(values, axis=-1, keepdims=True)
    centred = values - centre
    spread = jnp.mean(centred * centred, axis=-1, keepdims=True)
    return centred * lax.rsqrt(spread + EPSILON) * scale_vec + offset_vec


def rotate(values, cosine, sine_term):
    half_size = values.shape[-1] // 2
    turned = jnp.concatenate([-values[..., half_size:], values[..., :half_size]], axis=-1)
    return values * cosine + turned * sine_term


def rotary_tables(starts, head_size):
    half_size = head_size // 2
    freq_index = jnp.arange(half_size).astype(jnp.float32)
    inverse = jnp.exp(freq_index * (-math.log(10000.0) / half_size))
    angles = starts.astype(jnp.float32)[..., None] * inverse
    angles = jnp.concatenate([angles, angles], axis=-1)
    return (jnp.cos(angles), jnp.sin(angles))


def allowed_keys(length, live_count):
    places = jnp.arange(length)
    return (places[None, :] <= places[:, None]) & (places[None, :] < live_count)


def exact_gelu(values):
    return jax.nn.gelu(values, approximate=False)


def masked_scores(queries, key_rows, live_count):
    scores = jnp.einsum("qhd,khd->hqk", queries, key_rows, preferred_element_type=jnp.float32)
    allowed = allowed_keys(queries.shape[0], live_count)
    return jnp.where(allowed[None], scores, MASKED)


def attend_forward(packed):
    queries, key_rows, value_rows, live_count = packed
    scores = masked_scores(queries, key_rows, live_count)
    row_max = jnp.max(scores, axis=-1, keepdims=True)
    weights = jnp.exp(scores - row_max)
    row_total = jnp.sum(weights, axis=-1, keepdims=True)
    attention_probs = weights / row_total
    mixed_rows = jnp.einsum(
        "hqk,khd->qhd",
        attention_probs.astype(jnp.bfloat16),
        value_rows,
        preferred_element_type=jnp.float32,
    )
    return (mixed_rows.astype(jnp.bfloat16), row_max[..., 0] + jnp.log(row_total[..., 0]))


def attend_backward(packed):
    queries, key_rows, value_rows, live_count, log_total, out_grad = packed
    scores = masked_scores(queries, key_rows, live_count)
    attention_probs = jnp.exp(scores - log_total[..., None])
    prob_grad = jnp.einsum("qhd,khd->hqk", out_grad, value_rows, preferred_element_type=jnp.float32)
    inner_sum = jnp.sum(prob_grad * attention_probs, axis=-1, keepdims=True)
    score_grad = (attention_probs * (prob_grad - inner_sum)).astype(jnp.bfloat16)
    query_grad = jnp.einsum(
        "hqk,khd->qhd", score_grad, key_rows, preferred_element_type=jnp.float32
    )
    key_grad = jnp.einsum("hqk,qhd->khd", score_grad, queries, preferred_element_type=jnp.float32)
    value_grad = jnp.einsum(
        "hqk,qhd->khd",
        attention_probs.astype(jnp.bfloat16),
        out_grad,
        preferred_element_type=jnp.float32,
    )
    return (query_grad, key_grad, value_grad)


def run_layer(segments, seg_start, seg_count, cotangent, weights):
    seq_local, seg_len, model_width = segments.shape
    token_rows = seq_local * seg_len
    gain_one = weights[0].astype(jnp.float32)
    shift_one = weights[1].astype(jnp.float32)
    gain_two = weights[2].astype(jnp.float32)
    shift_two = weights[3].astype(jnp.float32)
    w_qkv, w_out, w_up = (weights[4], weights[5], weights[6])
    b_up = weights[7].astype(jnp.float32)
    w_down = weights[8]
    local_width = w_qkv.shape[2]
    local_heads = local_width // HEAD
    head_shape = (token_rows, local_heads, HEAD)
    seq_shape = (seq_local, seg_len, local_heads, HEAD)
    inputs = segments.reshape(token_rows, model_width).astype(jnp.float32)
    normed_one, norm_one_pull = jax.vjp(normalize, inputs, gain_one, shift_one)
    attn_in = normed_one.astype(jnp.bfloat16)
    projected = jnp.einsum("nd,dct->nct", attn_in, w_qkv, preferred_element_type=jnp.float32)
    cosine, sine_term = rotary_tables(seg_start.reshape(token_rows), HEAD)
    cosine = cosine[:, None, :]
    sine_term = sine_term[:, None, :]

    def place_rotary(raw_query, raw_key):
        return (
            rotate(raw_query, cosine, sine_term) * HEAD ** (-0.5),
            rotate(raw_key, cosine, sine_term),
        )

    rotated, rotary_pull = jax.vjp(
        place_rotary, projected[:, 0].reshape(head_shape), projected[:, 1].reshape(head_shape)
    )
    queries = rotated[0].astype(jnp.bfloat16).reshape(seq_shape)
    key_rows = rotated[1].astype(jnp.bfloat16).reshape(seq_shape)
    value_rows = projected[:, 2].astype(jnp.bfloat16).reshape(seq_shape)
    mixed_rows, log_total = lax.map(attend_forward, (queries, key_rows, value_rows, seg_count))
    mixed_flat = mixed_rows.reshape(token_rows, local_width)
    attn_part = jnp.dot(mixed_flat, w_out, preferred_element_type=jnp.float32)
    attn_full = lax.psum(attn_part, "tensor")
    residual = inputs + attn_full
    normed_two, norm_two_pull = jax.vjp(normalize, residual, gain_two, shift_two)
    ffn_in = normed_two.astype(jnp.bfloat16)
    pre_act = jnp.dot(ffn_in, w_up, preferred_element_type=jnp.float32) + b_up
    activated, gelu_pull = jax.vjp(exact_gelu, pre_act)
    act_low = activated.astype(jnp.bfloat16)
    ffn_part = jnp.dot(act_low, w_down, preferred_element_type=jnp.float32)
    ffn_full = lax.psum(ffn_part.astype(jnp.bfloat16), "tensor").astype(jnp.float32)
    block_out = (residual + ffn_full).astype(jnp.bfloat16).reshape(segments.shape)
    out_rows = cotangent.reshape(token_rows, model_width)
    down_grad = jnp.einsum("nf,nd->fd", act_low, out_rows, preferred_element_type=jnp.float32)
    act_grad = jnp.einsum("nd,fd->nf", out_rows, w_down, preferred_element_type=jnp.float32)
    pre_grad = gelu_pull(act_grad)[0].astype(jnp.bfloat16)
    bias_grad = jnp.sum(pre_grad, axis=0, dtype=jnp.float32)
    up_grad = jnp.einsum("nd,nf->df", ffn_in, pre_grad, preferred_element_type=jnp.float32)
    ffn_in_part = jnp.einsum("nf,df->nd", pre_grad, w_up, preferred_element_type=jnp.float32)
    ffn_in_grad = lax.psum(ffn_in_part, "tensor")
    resid_ln_grad, gain_two_grad, shift_two_grad = norm_two_pull(ffn_in_grad)
    residual_grad = out_rows.astype(jnp.float32) + resid_ln_grad
    attn_grad_low = residual_grad.astype(jnp.bfloat16)
    out_w_grad = jnp.einsum(
        "nt,nd->td", mixed_flat, attn_grad_low, preferred_element_type=jnp.float32
    )
    mixed_grad = jnp.einsum(
        "nd,td->nt", attn_grad_low, w_out, preferred_element_type=jnp.float32
    ).astype(jnp.bfloat16)
    ffn_shares = None
    query_grad, key_grad, value_grad = lax.map(
        attend_backward,
        (queries, key_rows, value_rows, seg_count, log_total, mixed_grad.reshape(seq_shape)),
    )
    raw_query_grad, raw_key_grad = rotary_pull(
        (query_grad.reshape(head_shape), key_grad.reshape(head_shape))
    )
    proj_grad = jnp.stack(
        [
            raw_query_grad.reshape(token_rows, local_width),
            raw_key_grad.reshape(token_rows, local_width),
            value_grad.reshape(token_rows, local_width),
        ],
        axis=1,
    ).astype(jnp.bfloat16)
    qkv_grad = jnp.einsum("nd,nct->dct", attn_in, proj_grad, preferred_element_type=jnp.float32)
    attn_in_part = jnp.einsum("nct,dct->nd", proj_grad, w_qkv, preferred_element_type=jnp.float32)
    attn_in_grad = lax.psum(attn_in_part.astype(jnp.bfloat16), "tensor").astype(jnp.float32)
    input_ln_grad, gain_one_grad, shift_one_grad = norm_one_pull(attn_in_grad)
    input_grad = (residual_grad + input_ln_grad).reshape(segments.shape)
    grads = (
        gain_one_grad,
        shift_one_grad,
        qkv_grad,
        out_w_grad,
        gain_two_grad,
        shift_two_grad,
        up_grad,
        bias_grad,
        down_grad,
    )
    return (block_out, input_grad, grads, ffn_shares)


def local(
    segments,
    seg_start,
    seg_count,
    norm_gain,
    norm_shift,
    qkv_weight,
    out_weight,
    ffn_gain,
    ffn_shift,
    up_weight,
    up_bias,
    down_weight,
    cotangent,
):
    gathered = (
        lax.all_gather(norm_gain, "dp", axis=0, tiled=True),
        lax.all_gather(norm_shift, "dp", axis=0, tiled=True),
        lax.all_gather(ffn_gain, "dp", axis=0, tiled=True),
        lax.all_gather(ffn_shift, "dp", axis=0, tiled=True),
        lax.all_gather(qkv_weight, "dp", axis=0, tiled=True),
        lax.all_gather(out_weight, "dp", axis=0, tiled=True),
        lax.all_gather(up_weight, "dp", axis=0, tiled=True),
        lax.all_gather(up_bias, "dp", axis=0, tiled=True),
        lax.all_gather(down_weight, "dp", axis=0, tiled=True),
    )
    block_out, input_grad, grads, ffn_shares = run_layer(
        segments, seg_start, seg_count, cotangent, gathered
    )
    (
        gain_one_grad,
        shift_one_grad,
        qkv_grad,
        out_w_grad,
        gain_two_grad,
        shift_two_grad,
        up_grad,
        bias_grad,
        down_grad,
    ) = grads
    shares = (
        summed_on_arrival(gain_one_grad.astype(jnp.bfloat16), "dp", 0),
        *sent_together(
            (shift_one_grad.astype(jnp.bfloat16), qkv_grad.astype(jnp.bfloat16)), "dp", 0, 1
        ),
        summed_on_arrival(out_w_grad.astype(jnp.bfloat16), "dp", 0),
        summed_on_arrival(gain_two_grad.astype(jnp.bfloat16), "dp", 0),
        *sent_together(
            (
                shift_two_grad.astype(jnp.bfloat16),
                up_grad.astype(jnp.bfloat16),
                bias_grad.astype(jnp.bfloat16),
                down_grad.astype(jnp.bfloat16),
            ),
            "dp",
            0,
            1,
        ),
    )
    gain_one_s, shift_one_s, qkv_s, out_s, gain_two_s, shift_two_s, up_s, bias_s, down_s = shares
    return (
        block_out,
        input_grad,
        gain_one_s,
        shift_one_s,
        qkv_s,
        out_s,
        gain_two_s,
        shift_two_s,
        up_s,
        bias_s,
        down_s,
    )


def solution(mesh):
    placed = (
        P("dp", None, None),
        P("dp", None),
        P("dp"),
        P("dp"),
        P("dp"),
        P("dp", None, "tensor"),
        P(("tensor", "dp"), None),
        P("dp"),
        P("dp"),
        P("dp", "tensor"),
        P(("tensor", "dp")),
        P(("tensor", "dp"), None),
        P("dp", None, None),
    )
    return jax.shard_map(
        local,
        mesh=mesh,
        in_specs=placed,
        out_specs=(
            P("dp", None, None),
            P("dp", None, None),
            P("dp"),
            P("dp"),
            P("dp", None, "tensor"),
            P(("tensor", "dp"), None),
            P("dp"),
            P("dp"),
            P("dp", "tensor"),
            P(("tensor", "dp")),
            P(("tensor", "dp"), None),
        ),
        check_vma=False,
    )
```

profile of v0, /device:TPU:0, one launch (start us, length us, event | category | flops | bytes accessed | tf_op | source)
XLA Modules:
  0.0 764.0 jit_solution(6756772383985416356)
XLA Ops:
  13.8 23.3 %all-reduce.9 = (bf16[512]{0:T(512)(128)(2,1)S(1)}, bf16[512]{0:T(512)(128)(2,1)S(1)}, bf16[512]{0:T(512)(128)(2,1)S(1)}, bf16[512]{0:T(512)(128)(2,1)S(1)}, bf16[512]{0:T(512)(128)(2,1)S(1)}) all-reduce(bf16[512]{0:T(512)(128)(2,1)S(1)} %dynamic-update-slice.1, ...), channel_id=1, replica_groups=mesh['dp'=8,'tensor'=4] {'dp'}, use_global_device_ids=true, to_apply=%add.5 | all-reduce | flops 2560 | bytes 10240
  37.3 31.0 %all_gather.29 = bf16[512,3,128]{2,0,1:T(8,128)(2,1)S(1)} all-gather(bf16[64,3,128]{2,0,1:T(8,128)(2,1)S(1)} %copy-done.44), channel_id=1, replica_groups=mesh['dp'=8,'tensor'=4] {'dp'}, dimensions={0}, use_global_device_ids=true | all-gather | bytes 442368 | tf_op jit(solution)/shard_map/all_gather | solution.py:228
  74.1 30.7 %all_gather.30 = bf16[128,512]{1,0:T(8,128)(2,1)S(1)} all-gather(bf16[16,512]{1,0:T(8,128)(2,1)S(1)} %copy-done.45), channel_id=1, replica_groups=mesh['dp'=8,'tensor'=4] {'dp'}, dimensions={0}, use_global_device_ids=true | all-gather | bytes 147456 | tf_op jit(solution)/shard_map/all_gather | solution.py:229
  104.9 6.5 fusion.85
  116.6 3.3 reshape_squeeze.10
  127.8 3.3 reshape_squeeze.12
  138.9 4.0 fusion.78
  144.9 31.6 %while.26 = (s32[]{:T(128)}, bf16[4,704,2,64]{1,3,2,0:T(8,128)(2,1)}, f32[4,2,704]{2,1,0:T(2,128)}, bf16[4,704,2,64]{1,3,2,0:T(8,128)(2,1)}, s32[4]{0:T(128)S(1)...) while((s32[]{:T(128)}, bf16[4,704,2,64]{1,3,2,0:T(8,128)(2,1)}, ...), condition=%wide.region_5.6_spmd, body=%wide.region_2.5_spmd.sunk | while | flops 263757120 | bytes 14712817 | solution.py:143
  181.9 4.6 fusion.97
  188.4 31.8 %all_gather.33 = bf16[512,512]{1,0:T(8,128)(2,1)S(1)} all-gather(bf16[64,512]{1,0:T(8,128)(2,1)} %param.26), channel_id=1, replica_groups=mesh['dp'=8,'tensor'=4] {'dp'}, dimensions={0}, use_global_device_ids=true | all-gather | bytes 589824 | tf_op jit(solution)/shard_map/all_gather | solution.py:230
  220.2 33.4 %all_gather.35 = bf16[512,512]{1,0:T(8,128)(2,1)} all-gather(bf16[64,512]{1,0:T(8,128)(2,1)} %param.28), channel_id=1, replica_groups=mesh['dp'=8,'tensor'=4] {'dp'}, dimensions={0}, use_global_device_ids=true | all-gather | bytes 589824 | tf_op jit(solution)/shard_map/all_gather | solution.py:232
  253.5 41.4 %all-reduce.15.cloned.1.call-done = f32[2816,512]{1,0:T(8,128)} async-done(((f32[2816,512]{1,0:T(8,128)}), f32[2816,512]{1,0:T(8,128)}) %all-reduce.15.cloned.1.call-update) | async-done | bytes 5767184 | tf_op jit(solution)/shard_map/psum | solution.py:146
  295.0 3.3 fusion.92
  303.4 16.5 %fusion.89 = (bf16[512]{0:T(512)(128)(2,1)}, bf16[2816,512]{1,0:T(8,128)(2,1)S(1)}, f32[2816,512]{1,0:T(8,128)}) fusion(f32[2816,512]{1,0:T(8,128)S(1)} %fusion.98, f32[512]{0:T(512)S(1)} %copy-done.48, bf16[2816,512]{1,0:T(8,128)(2,1)S(1)} %bitcast.198, bf16[512,512]{1,0:T(8,128)(2,1)S(1)} %copy-done.29), kind=kOutput, calls=%fused_computation.166 | convolution fusion | flops 1583087104 | bytes 17828864 | tf_op jit(solution)/shard_map/nd,fd->nf/dot_general | solution.py:158
  321.4 4.1 fusion.99
  326.4 3.8 broadcast_multiply_fusion.3
  330.1 7.0 multiply_convert_fusion.1
  337.2 3.3 convolution_convert_fusion
  343.1 93.9 %all-reduce.17.cloned.1.call-done = f32[2816,512]{1,0:T(8,128)} async-done(((f32[2816,512]{1,0:T(8,128)}), f32[2816,512]{1,0:T(8,128)}) %all-reduce.17.cloned.1.call-update) | async-done | bytes 5767184 | tf_op jit(solution)/shard_map/psum | solution.py:163
  437.0 6.3 multiply_reduce_fusion.1
  443.3 6.5 fusion.91
  450.4 5.5 all-to-all-start.3
  456.0 3.3 fusion.69
  463.4 3.4 copy.96
  466.9 106.9 %while.27 = (s32[]{:T(128)}, f32[4,704,2,64]{1,0,3,2:T(4,128)}, f32[4,704,2,64]{1,0,3,2:T(4,128)}, bf16[4,704,2,64]{1,3,2,0:T(8,128)(2,1)}, bf16[4,704,2,64]{1,3...) while((s32[]{:T(128)}, f32[4,704,2,64]{1,0,3,2:T(4,128)}, ...), condition=%wide.region_15.16_spmd, body=%wide.region_13.15_spmd.sunk | while | flops 647273792 | bytes 44077144 | solution.py:174
  476.8 8.4 %dynamic_update_slice.30 = f32[4,704,2,64]{1,0,3,2:T(4,128)} dynamic-update-slice(f32[4,704,2,64]{1,0,3,2:T(4,128)} %get-tuple-element.440, f32[1,704,2,64]{1,0,3,2:T(1,128)S(1)} %copy.151, s32[]{:T(128)S(6)} %copy.177, s32[]{:T(128)} %constant.60.clone.1..sunk, s32[]{:T(128)} %constant.60.clone.1..sunk, s32[]{:T(128)} %constant.60.clone.1..sunk) | dynamic-update-slice | bytes 720900 | tf_op jit(solution)/shard_map/while/body/jit(dynamic_update_index_in_dim)/dynamic_update_slice | solution.py:174
  485.2 8.4 %dynamic_update_slice.29 = f32[4,704,2,64]{1,0,3,2:T(4,128)} dynamic-update-slice(f32[4,704,2,64]{1,0,3,2:T(4,128)} %get-tuple-element.439, f32[1,704,2,64]{1,0,3,2:T(1,128)S(1)} %copy.150, s32[]{:T(128)S(6)} %copy.177, s32[]{:T(128)} %constant.60.clone.1..sunk, s32[]{:T(128)} %constant.60.clone.1..sunk, s32[]{:T(128)} %constant.60.clone.1..sunk) | dynamic-update-slice | bytes 720900 | tf_op jit(solution)/shard_map/while/body/jit(dynamic_update_index_in_dim)/dynamic_update_slice | solution.py:174
  503.5 8.4 %dynamic_update_slice.30 = f32[4,704,2,64]{1,0,3,2:T(4,128)} dynamic-update-slice(f32[4,704,2,64]{1,0,3,2:T(4,128)} %get-tuple-element.440, f32[1,704,2,64]{1,0,3,2:T(1,128)S(1)} %copy.151, s32[]{:T(128)S(6)} %copy.177, s32[]{:T(128)} %constant.60.clone.1..sunk, s32[]{:T(128)} %constant.60.clone.1..sunk, s32[]{:T(128)} %constant.60.clone.1..sunk) | dynamic-update-slice | bytes 720900 | tf_op jit(solution)/shard_map/while/body/jit(dynamic_update_index_in_dim)/dynamic_update_slice | solution.py:174
  511.9 8.4 %dynamic_update_slice.29 = f32[4,704,2,64]{1,0,3,2:T(4,128)} dynamic-update-slice(f32[4,704,2,64]{1,0,3,2:T(4,128)} %get-tuple-element.439, f32[1,704,2,64]{1,0,3,2:T(1,128)S(1)} %copy.150, s32[]{:T(128)S(6)} %copy.177, s32[]{:T(128)} %constant.60.clone.1..sunk, s32[]{:T(128)} %constant.60.clone.1..sunk, s32[]{:T(128)} %constant.60.clone.1..sunk) | dynamic-update-slice | bytes 720900 | tf_op jit(solution)/shard_map/while/body/jit(dynamic_update_index_in_dim)/dynamic_update_slice | solution.py:174
  530.2 8.4 %dynamic_update_slice.30 = f32[4,704,2,64]{1,0,3,2:T(4,128)} dynamic-update-slice(f32[4,704,2,64]{1,0,3,2:T(4,128)} %get-tuple-element.440, f32[1,704,2,64]{1,0,3,2:T(1,128)S(1)} %copy.151, s32[]{:T(128)S(6)} %copy.177, s32[]{:T(128)} %constant.60.clone.1..sunk, s32[]{:T(128)} %constant.60.clone.1..sunk, s32[]{:T(128)} %constant.60.clone.1..sunk) | dynamic-update-slice | bytes 720900 | tf_op jit(solution)/shard_map/while/body/jit(dynamic_update_index_in_dim)/dynamic_update_slice | solution.py:174
  538.6 8.4 %dynamic_update_slice.29 = f32[4,704,2,64]{1,0,3,2:T(4,128)} dynamic-update-slice(f32[4,704,2,64]{1,0,3,2:T(4,128)} %get-tuple-element.439, f32[1,704,2,64]{1,0,3,2:T(1,128)S(1)} %copy.150, s32[]{:T(128)S(6)} %copy.177, s32[]{:T(128)} %constant.60.clone.1..sunk, s32[]{:T(128)} %constant.60.clone.1..sunk, s32[]{:T(128)} %constant.60.clone.1..sunk) | dynamic-update-slice | bytes 720900 | tf_op jit(solution)/shard_map/while/body/jit(dynamic_update_index_in_dim)/dynamic_update_slice | solution.py:174
  556.9 8.4 %dynamic_update_slice.30 = f32[4,704,2,64]{1,0,3,2:T(4,128)} dynamic-update-slice(f32[4,704,2,64]{1,0,3,2:T(4,128)} %get-tuple-element.440, f32[1,704,2,64]{1,0,3,2:T(1,128)S(1)} %copy.151, s32[]{:T(128)S(6)} %copy.177, s32[]{:T(128)} %constant.60.clone.1..sunk, s32[]{:T(128)} %constant.60.clone.1..sunk, s32[]{:T(128)} %constant.60.clone.1..sunk) | dynamic-update-slice | bytes 720900 | tf_op jit(solution)/shard_map/while/body/jit(dynamic_update_index_in_dim)/dynamic_update_slice | solution.py:174
  565.3 8.4 %dynamic_update_slice.29 = f32[4,704,2,64]{1,0,3,2:T(4,128)} dynamic-update-slice(f32[4,704,2,64]{1,0,3,2:T(4,128)} %get-tuple-element.439, f32[1,704,2,64]{1,0,3,2:T(1,128)S(1)} %copy.150, s32[]{:T(128)S(6)} %copy.177, s32[]{:T(128)} %constant.60.clone.1..sunk, s32[]{:T(128)} %constant.60.clone.1..sunk, s32[]{:T(128)} %constant.60.clone.1..sunk) | dynamic-update-slice | bytes 720900 | tf_op jit(solution)/shard_map/while/body/jit(dynamic_update_index_in_dim)/dynamic_update_slice | solution.py:174
  573.8 3.9 copy.119
  593.0 4.5 bitcast_convert_fusion
  601.6 6.0 all-to-all-start.2
  607.6 5.2 convolution_convert_fusion.2
  615.4 3.5 concatenate.60
  619.0 6.0 all-to-all-start.4
  631.7 20.8 %all-to-all-done.4 = bf16[8,64,1026]{2,1,0:T(8,128)(2,1)} async-done(((bf16[8,64,1026]{2,1,0:T(8,128)(2,1)}), bf16[8,64,1026]{2,1,0:T(8,128)(2,1)}, u32[]{:S(2)}, u32[]{:S(2)}) %all-to-all-start.4) | async-done | bytes 1050656 | tf_op jit(solution)/shard_map/all_to_all | solution.py:20
  655.6 54.0 %all-reduce.19.cloned.1.call-done = (bf16[2816,512]{1,0:T(8,128)(2,1)}, bf16[2816,512]{1,0:T(8,128)(2,1)}) async-done(((bf16[2816,512]{1,0:T(8,128)(2,1)}, bf16[2816,512]{1,0:T(8,128)(2,1)}), (bf16[2816,512]{1,0:T(8,128)(2,1)}, bf16[2816,512]{1,0:T(8,128)(2,1)})) %all-reduce.19.cloned.1.call-update) | async-done | bytes 5767184 | tf_op jit(solution)/shard_map/psum | solution.py:154
  709.6 3.4 fusion.53
  715.2 4.8 fusion.54
  720.7 5.8 all-to-all-start
  726.5 8.1 %add_add_fusion.2 = f32[2816,512]{1,0:T(8,128)} fusion(bf16[4,704,512]{2,1,0:T(8,128)(2,1)S(1)} %copy-done.2, bf16[2816,512]{1,0:T(8,128)(2,1)} %get-tuple-element.256, f32[2816,512]{1,0:T(8,128)} %get-tuple-element.261, f32[2816]{0:T(1024)S(1)} %negate_multiply_fusion.1, f32[2816]{0:T(1024)S(1)} %multiply_multiply_fusion.5, ...), kind=kLoop, calls=%fused_computation.83 | loop fusion | flops 18743296 | bytes 20243456 | tf_op jit(solution)/shard_map/add | solution.py:193
  736.0 6.0 all-to-all-start.1
  742.0 6.1 add_convert_fusion.1
  748.6 7.1 all-to-all-done.1
  (306 shorter events, 165.0 us)
Async XLA Ops:
  7.2 4.1 copy-start.58
  7.2 5.3 copy-start.51
  7.2 5.6 copy-start.52
  7.2 5.8 copy-start.53
  7.2 6.1 copy-start.54
  7.2 6.3 copy-start.55
  7.3 30.0 %copy-start.44 = (bf16[64,3,128]{2,0,1:T(8,128)(2,1)S(1)}, bf16[64,3,128]{2,0,1:T(8,128)(2,1)}, u32[]{:S(2)}) copy-start(bf16[64,3,128]{2,0,1:T(8,128)(2,1)} %param.22) | copy-start | bytes 147460
  7.3 287.7 %all-reduce.15.cloned.1.call-start = ((), (), s32[]{:S(2)}) async-start(), calls=%async_computation.5 | async-start | bytes 11534336 | tf_op jit(solution)/shard_map/psum | solution.py:146
  7.3 97.5 %copy-start.49 = (f32[32]{0:T(128)}, f32[32]{0:T(128)S(1)}, u32[]{:S(2)}) copy-start(f32[32]{0:T(128)S(1)} %multiply_exponential_fusion) | copy-start | bytes 388
  9.9 60.0 %copy-start.31 = (f32[2816]{0:T(1024)}, f32[2816]{0:T(1024)S(1)}, u32[]{:S(2)}) copy-start(f32[2816]{0:T(1024)S(1)} %div.47) | copy-start | bytes 33796
  37.1 34.2 %copy-start.41 = (f32[512]{0:T(512)}, f32[512]{0:T(512)S(1)}, u32[]{:S(2)}) copy-start(f32[512]{0:T(512)S(1)} %convert_element_type.198) | copy-start | bytes 6148
  37.3 34.1 %copy-start.37 = (f32[2816]{0:T(1024)}, f32[2816]{0:T(1024)S(1)}, u32[]{:S(2)}) copy-start(f32[2816]{0:T(1024)S(1)} %add.103) | copy-start | bytes 33796
  37.3 31.1 %copy-start.33 = (f32[2816]{0:T(1024)}, f32[2816]{0:T(1024)S(1)}, u32[]{:S(2)}) copy-start(f32[2816]{0:T(1024)S(1)} %rsqrt.20) | copy-start | bytes 33796
  68.3 3.0 copy-start.22
  138.9 6.0 copy-start.56
  186.5 250.5 %all-reduce.17.cloned.1.call-start = ((), (), s32[]{:S(2)}) async-start(), calls=%async_computation.6 | async-start | bytes 11534336 | tf_op jit(solution)/shard_map/psum | solution.py:163
  298.3 3.2 copy-start
  303.2 16.7 %copy-start.5 = (f32[2816,512]{1,0:T(8,128)}, f32[2816,512]{1,0:T(8,128)S(1)}, u32[]{:S(2)}) copy-start(f32[2816,512]{1,0:T(8,128)S(1)} %fusion.98) | copy-start | bytes 17301508
  330.1 7.0 copy-start.30
  337.2 3.3 copy-start.20
  337.2 3.5 copy-start.14
  340.6 96.4 %copy-start.36 = (f32[2816]{0:T(1024)S(1)}, f32[2816]{0:T(1024)}, u32[]{:S(2)}) copy-start(f32[2816]{0:T(1024)} %copy-done.35) | copy-start | bytes 33796
  343.1 100.2 %copy-start.40 = (f32[2816]{0:T(1024)S(1)}, f32[2816]{0:T(1024)}, u32[]{:S(2)}) copy-start(f32[2816]{0:T(1024)} %copy-done.39) | copy-start | bytes 33796
  437.0 6.3 copy-start.6
  443.3 12.7 %copy-start.10 = (bf16[4,704,512]{2,1,0:T(8,128)(2,1)S(1)}, bf16[4,704,512]{2,1,0:T(8,128)(2,1)}, u32[]{:S(2)}) copy-start(bf16[4,704,512]{2,1,0:T(8,128)(2,1)} %param.29) | copy-start | bytes 8650756
  450.4 151.2 %all-to-all-start.3 = ((bf16[8,1,64]{2,1,0:T(2,128)(2,1)}), bf16[8,1,64]{2,1,0:T(2,128)(2,1)S(1)}, u32[]{:S(2)}, u32[]{:S(2)}) async-start(bf16[8,1,64]{2,1,0:T(2,128)(2,1)} %convert_element_type.240), calls=%async_computation.3 | async-start | bytes 8192 | tf_op jit(solution)/shard_map/all_to_all | solution.py:20
  456.0 253.6 %all-reduce.19.cloned.1.call-start = ((), (), s32[]{:S(2)}) async-start(), calls=%async_computation.7 | async-start | bytes 11534336 | tf_op jit(solution)/shard_map/psum | solution.py:154
  460.9 5.9 copy-start.7
  460.9 5.9 copy-start.8
  460.9 5.9 copy-start.57
  466.9 3.0 copy-start.24
  493.6 3.0 copy-start.24
  520.4 3.0 copy-start.24
  547.1 3.0 copy-start.24
  573.8 7.7 %copy-start.15 = (f32[2816,64]{0,1:T(8,128)S(1)}, f32[2816,64]{0,1:T(8,128)}, u32[]{:S(2)}) copy-start(f32[2816,64]{0,1:T(8,128)} %get-tuple-element.283) | copy-start | bytes 2162692
  587.3 5.7 copy-start.23
  601.6 17.4 %all-to-all-start.2 = ((bf16[8,16,512]{2,1,0:T(8,128)(2,1)}), bf16[8,16,512]{2,1,0:T(8,128)(2,1)}, u32[]{:S(2)}, u32[]{:S(2)}) async-start(bf16[8,16,512]{2,1,0:T(8,128)(2,1)} %bitcast.31), calls=%async_computation.2 | async-start | bytes 262144 | tf_op jit(solution)/shard_map/all_to_all | solution.py:20
  607.5 7.9 %copy-start.28 = (bf16[512,512]{1,0:T(8,128)(2,1)S(1)}, bf16[512,512]{1,0:T(8,128)(2,1)}, u32[]{:S(2)}) copy-start(bf16[512,512]{1,0:T(8,128)(2,1)} %convolution_convert_fusion.3) | copy-start | bytes 1572868
  612.8 12.2 %copy-start.12 = (bf16[2816,512]{1,0:T(8,128)(2,1)S(1)}, bf16[2816,512]{1,0:T(8,128)(2,1)}, u32[]{:S(2)}) copy-start(bf16[2816,512]{1,0:T(8,128)(2,1)} %copy-done.11) | copy-start | bytes 8650756
  619.0 33.6 %all-to-all-start.4 = ((bf16[8,64,1026]{2,1,0:T(8,128)(2,1)}), bf16[8,64,1026]{2,1,0:T(8,128)(2,1)}, u32[]{:S(2)}, u32[]{:S(2)}) async-start(bf16[8,64,1026]{2,1,0:T(8,128)(2,1)} %concatenate.60), calls=%async_computation.4 | async-start | bytes 2359296 | tf_op jit(solution)/shard_map/all_to_all | solution.py:20
  624.9 84.6 %copy-start.32 = (f32[2816]{0:T(1024)S(1)}, f32[2816]{0:T(1024)}, u32[]{:S(2)}) copy-start(f32[2816]{0:T(1024)} %copy-done.31) | copy-start | bytes 33796
  625.0 84.6 %copy-start.42 = (f32[512]{0:T(512)S(1)}, f32[512]{0:T(512)}, u32[]{:S(2)}) copy-start(f32[512]{0:T(512)} %copy-done.41) | copy-start | bytes 6148
  628.2 81.4 %copy-start.2 = (bf16[4,704,512]{2,1,0:T(8,128)(2,1)S(1)}, bf16[4,704,512]{2,1,0:T(8,128)(2,1)}, u32[]{:S(2)}) copy-start(bf16[4,704,512]{2,1,0:T(8,128)(2,1)} %param.17) | copy-start | bytes 8650756
  709.6 5.7 copy-start.38
  709.6 5.7 copy-start.34
  720.7 15.3 %all-to-all-start = ((bf16[8,1,64]{2,1,0:T(2,128)(2,1)}), bf16[8,1,64]{2,1,0:T(2,128)(2,1)S(1)}, u32[]{:S(2)}, u32[]{:S(2)}) async-start(bf16[8,1,64]{2,1,0:T(2,128)(2,1)} %convert_element_type.238), calls=%async_computation | async-start | bytes 8192 | tf_op jit(solution)/shard_map/all_to_all | solution.py:20
  726.5 8.3 %copy-start.21 = (bf16[8,64,384]{2,1,0:T(8,128)(2,1)S(1)}, bf16[8,64,384]{2,1,0:T(8,128)(2,1)}, u32[]{:S(2)}) copy-start(bf16[8,64,384]{2,1,0:T(8,128)(2,1)} %concatenate.55) | copy-start | bytes 1179652
  736.0 19.8 %all-to-all-start.1 = ((bf16[8,64,385]{2,1,0:T(8,128)(2,1)}), bf16[8,64,385]{2,1,0:T(8,128)(2,1)S(1)}, u32[]{:S(2)}, u32[]{:S(2)}) async-start(bf16[8,64,385]{2,1,0:T(8,128)(2,1)} %pad_maximum_fusion.5), calls=%async_computation.1 | async-start | bytes 1048576 | tf_op jit(solution)/shard_map/all_to_all | solution.py:20
  (25 other events, 47.4 us)
Sparse Core Ops, SparseCore 0:
  186.6 108.3 all-reduce.14
  325.7 111.2 all-reduce.16
  597.6 111.8 all-reduce.18
where the time goes:
time: 773 us; the launch traced here: 764 us
  waiting for transfers between devices  217 us (28%)
  local copies, waits for them, and re-layouts  151 us (20%)
  blocking collectives  150 us (19%)
  other arithmetic  107 us (14%)
  matrix products  92.4 us (12%)
  starting transfers between devices  29.4 us (4%)
  between operations  15.5 us (2%)
    psum x1, waiting for transfers between devices, run_layer(): ffn_in_grad = lax.psum(ffn_in_part, 'tensor')  93.9 us
    dynamic_update_slice x16, local copies, waits for them, and re-layouts, run_layer(): lax.map(attend_backward, (queries, key_rows, value_rows, seg_count, log_t...  70.8 us
    psum x1, waiting for transfers between devices, run_layer(): lax.psum(ffn_part.astype(jnp.bfloat16), 'tensor').astype(jnp.float32)  54 us
    psum x1, waiting for transfers between devices, run_layer(): attn_full = lax.psum(attn_part, 'tensor')  41.4 us
    all_gather x1, blocking collectives, local(): lax.all_gather(down_weight, 'dp', axis=0, tiled=True)  33.4 us
    all_gather x1, blocking collectives, local(): lax.all_gather(up_weight, 'dp', axis=0, tiled=True)  31.8 us
    all_gather x1, blocking collectives, local(): lax.all_gather(qkv_weight, 'dp', axis=0, tiled=True)  31 us
    all_gather x1, blocking collectives, local(): lax.all_gather(out_weight, 'dp', axis=0, tiled=True)  30.7 us
  transfers between devices with their start and end apart: 8, of which 5 were waited for; matrix products, arithmetic and copies ran while one was open for 26% of the time, Pallas kernels for 0%

commit v1 on v0

--- a/solution.py
+++ b/solution.py
@@ -143,7 +143,7 @@
     mixed_rows, log_total = lax.map(attend_forward, (queries, key_rows, value_rows, seg_count))
     mixed_flat = mixed_rows.reshape(token_rows, local_width)
     attn_part = jnp.dot(mixed_flat, w_out, preferred_element_type=jnp.float32)
-    attn_full = lax.psum(attn_part, "tensor")
+    attn_full = jnp.sum(lax.all_gather(attn_part, "tensor"), axis=0)
     residual = inputs + attn_full
     normed_two, norm_two_pull = jax.vjp(normalize, residual, gain_two, shift_two)
     ffn_in = normed_two.astype(jnp.bfloat16)

time: 773 us -> 848 us (1.097)
  waiting for transfers between devices: 217 us -> 247 us
  matrix products: 92.4 us -> 117 us
  other arithmetic: 107 us -> 121 us
  local copies, waits for them, and re-layouts: 151 us -> 162 us
    all_gather x0 -> x1, waiting for transfers between devices: none -> 73.5 us  [run_layer(): attn_full = jnp.sum(lax.all_gather(attn_part, 'tensor'), axis=0)]
    psum x1 -> x0, waiting for transfers between devices: 41.4 us -> none  [run_layer(): attn_full = lax.psum(attn_part, 'tensor')]
    reduce_sum x0 -> x1, other arithmetic: none -> 14.3 us  [run_layer(): attn_full = jnp.sum(lax.all_gather(attn_part, 'tensor'), axis=0)]
    dot_general x4, matrix products: 4.6 us -> 16.7 us  [attend_backward(): jnp.einsum('hqk,qhd->khd', attention_probs.astype(jnp.bfloat16), out_grad...]
  transfers between devices with their start and end apart: 8 -> 8, of which waited for: 5 -> 6; matrix products, arithmetic and copies ran while one was open for 26% -> 7% of each run, Pallas kernels for 0% -> 0%
where the time goes in v1:
time: 848 us; the launch traced here: 840 us
  waiting for transfers between devices  247 us (29%)
  local copies, waits for them, and re-layouts  162 us (19%)
  blocking collectives  150 us (18%)
  other arithmetic  121 us (14%)
  matrix products  117 us (14%)
  starting transfers between devices  27 us (3%)
  between operations  15.5 us (2%)
    psum x1, waiting for transfers between devices, run_layer(): ffn_in_grad = lax.psum(ffn_in_part, 'tensor')  92.3 us
    all_gather x1, waiting for transfers between devices, run_layer(): attn_full = jnp.sum(lax.all_gather(attn_part, 'tensor'), axis=0)  73.5 us
    dynamic_update_slice x16, local copies, waits for them, and re-layouts, run_layer(): lax.map(attend_backward, (queries, key_rows, value_rows, seg_count, log_t...  70.7 us
    psum x1, waiting for transfers between devices, run_layer(): lax.psum(ffn_part.astype(jnp.bfloat16), 'tensor').astype(jnp.float32)  53.9 us
    all_gather x1, blocking collectives, local(): lax.all_gather(down_weight, 'dp', axis=0, tiled=True)  33.4 us
    all_gather x1, blocking collectives, local(): lax.all_gather(up_weight, 'dp', axis=0, tiled=True)  31.8 us
    all_gather x1, blocking collectives, local(): lax.all_gather(qkv_weight, 'dp', axis=0, tiled=True)  31.1 us
    all_gather x1, blocking collectives, local(): lax.all_gather(out_weight, 'dp', axis=0, tiled=True)  30.6 us
  transfers between devices with their start and end apart: 8, of which 6 were waited for; matrix products, arithmetic and copies ran while one was open for 7% of the time, Pallas kernels for 0%

profile of v1, /device:TPU:0, one launch (start us, length us, event | category | flops | bytes accessed | tf_op | source)
XLA Modules:
  0.0 840.2 jit_solution(8690211813706925747)
XLA Ops:
  15.5 23.4 %all-reduce.9 = (bf16[512]{0:T(512)(128)(2,1)S(1)}, bf16[512]{0:T(512)(128)(2,1)S(1)}, bf16[512]{0:T(512)(128)(2,1)S(1)}, bf16[512]{0:T(512)(128)(2,1)S(1)}, bf16[512]{0:T(512)(128)(2,1)S(1)}) all-reduce(bf16[512]{0:T(512)(128)(2,1)S(1)} %dynamic-update-slice.3, ...), channel_id=1, replica_groups=mesh['dp'=8,'tensor'=4] {'dp'}, use_global_device_ids=true, to_apply=%add.7 | all-reduce | flops 2560 | bytes 10240
  39.0 31.1 %all_gather.35 = bf16[512,3,128]{2,0,1:T(8,128)(2,1)S(1)} all-gather(bf16[64,3,128]{2,0,1:T(8,128)(2,1)S(1)} %copy-done.42), channel_id=1, replica_groups=mesh['dp'=8,'tensor'=4] {'dp'}, dimensions={0}, use_global_device_ids=true | all-gather | bytes 442368 | tf_op jit(solution)/shard_map/all_gather | solution.py:228
  98.3 5.6 fusion.86
  104.0 3.6 fusion.79
  114.8 31.6 %while.26 = (s32[]{:T(128)}, bf16[4,704,2,64]{1,3,2,0:T(8,128)(2,1)}, f32[4,2,704]{2,1,0:T(2,128)}, bf16[4,704,2,64]{1,3,2,0:T(8,128)(2,1)}, s32[4]{0:T(128)S(1)...) while((s32[]{:T(128)}, bf16[4,704,2,64]{1,3,2,0:T(8,128)(2,1)}, ...), condition=%wide.region_5.6_spmd, body=%wide.region_2.5_spmd.sunk | while | flops 263757120 | bytes 14713317 | solution.py:143
  151.7 30.6 %all_gather.36 = bf16[128,512]{1,0:T(8,128)(2,1)S(1)} all-gather(bf16[16,512]{1,0:T(8,128)(2,1)S(1)} %copy-done.43), channel_id=1, replica_groups=mesh['dp'=8,'tensor'=4] {'dp'}, dimensions={0}, use_global_device_ids=true | all-gather | bytes 147456 | tf_op jit(solution)/shard_map/all_gather | solution.py:229
  182.3 4.6 fusion.96
  188.8 31.8 %all_gather.41 = bf16[512,512]{1,0:T(8,128)(2,1)S(1)} all-gather(bf16[64,512]{1,0:T(8,128)(2,1)} %param.26), channel_id=1, replica_groups=mesh['dp'=8,'tensor'=4] {'dp'}, dimensions={0}, use_global_device_ids=true | all-gather | bytes 589824 | tf_op jit(solution)/shard_map/all_gather | solution.py:230
  220.7 33.4 %all_gather.43 = bf16[512,512]{1,0:T(8,128)(2,1)} all-gather(bf16[64,512]{1,0:T(8,128)(2,1)} %param.28), channel_id=1, replica_groups=mesh['dp'=8,'tensor'=4] {'dp'}, dimensions={0}, use_global_device_ids=true | all-gather | bytes 589824 | tf_op jit(solution)/shard_map/all_gather | solution.py:232
  254.1 73.5 %all-gather.3.cloned.1.call-done = f32[11264,512]{1,0:T(8,128)} async-done(((f32[2816,512]{1,0:T(8,128)}), f32[11264,512]{1,0:T(8,128)}) %all-gather.3.cloned.1.call-update) | async-done | bytes 23068688 | tf_op jit(solution)/shard_map/all_gather | solution.py:146
  327.6 14.3 %reduce_sum.204 = f32[2816,512]{1,0:T(8,128)} reduce(f32[4,2816,512]{2,1,0:T(8,128)} %bitcast.209, f32[]{:T(128)} %constant.62.clone.1), dimensions={0}, to_apply=%region_6.7 | reduce | flops 4325376 | bytes 28835844 | tf_op jit(solution)/shard_map/reduce_sum | solution.py:146
  353.1 3.6 add_convert_fusion.2
  360.5 16.5 %fusion.89 = (bf16[512]{0:T(512)(128)(2,1)}, bf16[2816,512]{1,0:T(8,128)(2,1)S(1)}, f32[2816,512]{1,0:T(8,128)}) fusion(f32[2816,512]{1,0:T(8,128)S(1)} %fusion.97, f32[512]{0:T(512)S(1)} %copy-done.45, bf16[2816,512]{1,0:T(8,128)(2,1)S(1)} %bitcast.213, bf16[512,512]{1,0:T(8,128)(2,1)S(1)} %copy-done.27), kind=kOutput, calls=%fused_computation.167 | convolution fusion | flops 1583087104 | bytes 17828864 | tf_op jit(solution)/shard_map/nd,fd->nf/dot_general | solution.py:158
  378.6 4.2 fusion.98
  383.6 3.9 broadcast_multiply_fusion.3
  387.5 6.9 multiply_convert_fusion.1
  401.7 92.3 %all-reduce.14.cloned.1.call-done = f32[2816,512]{1,0:T(8,128)} async-done(((f32[2816,512]{1,0:T(8,128)}), f32[2816,512]{1,0:T(8,128)}) %all-reduce.14.cloned.1.call-update) | async-done | bytes 5767184 | tf_op jit(solution)/shard_map/psum | solution.py:163
  494.1 6.4 multiply_reduce_fusion.1
  500.5 5.0 fusion.91
  509.7 3.8 reshape.461
  513.5 4.7 copy.96
  518.2 130.6 %while.27 = (s32[]{:T(128)}, f32[4,704,2,64]{1,0,3,2:T(4,128)}, f32[4,704,2,64]{1,0,3,2:T(4,128)}, bf16[4,704,2,64]{1,3,2,0:T(8,128)(2,1)}, bf16[4,704,2,64]{1,3...) while((s32[]{:T(128)}, f32[4,704,2,64]{1,0,3,2:T(4,128)}, ...), condition=%wide.region_15.16_spmd, body=%wide.region_13.15_spmd.sunk | while | flops 647273792 | bytes 53358636 | solution.py:174
  528.1 8.4 %dynamic_update_slice.30 = f32[4,704,2,64]{1,0,3,2:T(4,128)} dynamic-update-slice(f32[4,704,2,64]{1,0,3,2:T(4,128)} %get-tuple-element.440, f32[1,704,2,64]{1,0,3,2:T(1,128)S(1)} %copy.152, s32[]{:T(128)} %get-tuple-element.438, s32[]{:T(128)} %constant.60.clone.1..sunk, s32[]{:T(128)} %constant.60.clone.1..sunk, s32[]{:T(128)} %constant.60.clone.1..sunk) | dynamic-update-slice | bytes 720900 | tf_op jit(solution)/shard_map/while/body/jit(dynamic_update_index_in_dim)/dynamic_update_slice | solution.py:174
  538.4 8.4 %dynamic_update_slice.29 = f32[4,704,2,64]{1,0,3,2:T(4,128)} dynamic-update-slice(f32[4,704,2,64]{1,0,3,2:T(4,128)} %get-tuple-element.439, f32[1,704,2,64]{1,0,3,2:T(1,128)S(1)} %copy.151, s32[]{:T(128)} %get-tuple-element.438, s32[]{:T(128)} %constant.60.clone.1..sunk, s32[]{:T(128)} %constant.60.clone.1..sunk, s32[]{:T(128)} %constant.60.clone.1..sunk) | dynamic-update-slice | bytes 720900 | tf_op jit(solution)/shard_map/while/body/jit(dynamic_update_index_in_dim)/dynamic_update_slice | solution.py:174
  546.8 4.2 fusion.150
  560.7 8.4 %dynamic_update_slice.30 = f32[4,704,2,64]{1,0,3,2:T(4,128)} dynamic-update-slice(f32[4,704,2,64]{1,0,3,2:T(4,128)} %get-tuple-element.440, f32[1,704,2,64]{1,0,3,2:T(1,128)S(1)} %copy.152, s32[]{:T(128)} %get-tuple-element.438, s32[]{:T(128)} %constant.60.clone.1..sunk, s32[]{:T(128)} %constant.60.clone.1..sunk, s32[]{:T(128)} %constant.60.clone.1..sunk) | dynamic-update-slice | bytes 720900 | tf_op jit(solution)/shard_map/while/body/jit(dynamic_update_index_in_dim)/dynamic_update_slice | solution.py:174
  571.0 8.4 %dynamic_update_slice.29 = f32[4,704,2,64]{1,0,3,2:T(4,128)} dynamic-update-slice(f32[4,704,2,64]{1,0,3,2:T(4,128)} %get-tuple-element.439, f32[1,704,2,64]{1,0,3,2:T(1,128)S(1)} %copy.151, s32[]{:T(128)} %get-tuple-element.438, s32[]{:T(128)} %constant.60.clone.1..sunk, s32[]{:T(128)} %constant.60.clone.1..sunk, s32[]{:T(128)} %constant.60.clone.1..sunk) | dynamic-update-slice | bytes 720900 | tf_op jit(solution)/shard_map/while/body/jit(dynamic_update_index_in_dim)/dynamic_update_slice | solution.py:174
  579.4 4.2 fusion.150
  593.3 8.4 %dynamic_update_slice.30 = f32[4,704,2,64]{1,0,3,2:T(4,128)} dynamic-update-slice(f32[4,704,2,64]{1,0,3,2:T(4,128)} %get-tuple-element.440, f32[1,704,2,64]{1,0,3,2:T(1,128)S(1)} %copy.152, s32[]{:T(128)} %get-tuple-element.438, s32[]{:T(128)} %constant.60.clone.1..sunk, s32[]{:T(128)} %constant.60.clone.1..sunk, s32[]{:T(128)} %constant.60.clone.1..sunk) | dynamic-update-slice | bytes 720900 | tf_op jit(solution)/shard_map/while/body/jit(dynamic_update_index_in_dim)/dynamic_update_slice | solution.py:174
  603.6 8.4 %dynamic_update_slice.29 = f32[4,704,2,64]{1,0,3,2:T(4,128)} dynamic-update-slice(f32[4,704,2,64]{1,0,3,2:T(4,128)} %get-tuple-element.439, f32[1,704,2,64]{1,0,3,2:T(1,128)S(1)} %copy.151, s32[]{:T(128)} %get-tuple-element.438, s32[]{:T(128)} %constant.60.clone.1..sunk, s32[]{:T(128)} %constant.60.clone.1..sunk, s32[]{:T(128)} %constant.60.clone.1..sunk) | dynamic-update-slice | bytes 720900 | tf_op jit(solution)/shard_map/while/body/jit(dynamic_update_index_in_dim)/dynamic_update_slice | solution.py:174
  612.0 4.2 fusion.150
  625.9 8.4 %dynamic_update_slice.30 = f32[4,704,2,64]{1,0,3,2:T(4,128)} dynamic-update-slice(f32[4,704,2,64]{1,0,3,2:T(4,128)} %get-tuple-element.440, f32[1,704,2,64]{1,0,3,2:T(1,128)S(1)} %copy.152, s32[]{:T(128)} %get-tuple-element.438, s32[]{:T(128)} %constant.60.clone.1..sunk, s32[]{:T(128)} %constant.60.clone.1..sunk, s32[]{:T(128)} %constant.60.clone.1..sunk) | dynamic-update-slice | bytes 720900 | tf_op jit(solution)/shard_map/while/body/jit(dynamic_update_index_in_dim)/dynamic_update_slice | solution.py:174
  636.2 8.4 %dynamic_update_slice.29 = f32[4,704,2,64]{1,0,3,2:T(4,128)} dynamic-update-slice(f32[4,704,2,64]{1,0,3,2:T(4,128)} %get-tuple-element.439, f32[1,704,2,64]{1,0,3,2:T(1,128)S(1)} %copy.151, s32[]{:T(128)} %get-tuple-element.438, s32[]{:T(128)} %constant.60.clone.1..sunk, s32[]{:T(128)} %constant.60.clone.1..sunk, s32[]{:T(128)} %constant.60.clone.1..sunk) | dynamic-update-slice | bytes 720900 | tf_op jit(solution)/shard_map/while/body/jit(dynamic_update_index_in_dim)/dynamic_update_slice | solution.py:174
  644.6 4.2 fusion.150
  663.6 3.8 copy.119
  669.5 5.5 all-to-all-start.3
  675.3 4.6 bitcast_convert_fusion
  684.0 6.1 all-to-all-start.2
  690.1 5.3 convolution_convert_fusion.2
  697.9 3.5 concatenate.60
  701.5 6.0 all-to-all-start.4
  714.3 20.8 %all-to-all-done.4 = bf16[8,64,1026]{2,1,0:T(8,128)(2,1)} async-done(((bf16[8,64,1026]{2,1,0:T(8,128)(2,1)}), bf16[8,64,1026]{2,1,0:T(8,128)(2,1)}, u32[]{:S(2)}, u32[]{:S(2)}) %all-to-all-start.4) | async-done | bytes 1050656 | tf_op jit(solution)/shard_map/all_to_all | solution.py:20
  738.1 53.9 %all-reduce.16.cloned.1.call-done = (bf16[2816,512]{1,0:T(8,128)(2,1)}, bf16[2816,512]{1,0:T(8,128)(2,1)}) async-done(((bf16[2816,512]{1,0:T(8,128)(2,1)}, bf16[2816,512]{1,0:T(8,128)(2,1)}), (bf16[2816,512]{1,0:T(8,128)(2,1)}, bf16[2816,512]{1,0:T(8,128)(2,1)})) %all-reduce.16.cloned.1.call-update) | async-done | bytes 5767184 | tf_op jit(solution)/shard_map/psum | solution.py:154
  798.0 4.8 fusion.54
  803.5 5.5 all-to-all-start
  810.1 5.3 all-to-all-done
  815.4 3.5 all-to-all-start.1
  818.9 11.1 %add_add_fusion.2 = (f32[2816,512]{1,0:T(8,128)}, bf16[2816,512]{1,0:T(8,128)(2,1)}) fusion(bf16[4,704,512]{2,1,0:T(8,128)(2,1)S(1)} %copy-done.2, bf16[2816,512]{1,0:T(8,128)(2,1)} %get-tuple-element.256, f32[2816,512]{1,0:T(8,128)} %copy-done.4, f32[2816]{0:T(1024)S(1)} %negate_multiply_fusion.1, f32[2816]{0:T(1024)S(1)} %multiply_multiply_fusion.5, ...), kind=kLoop, calls=%fused_computation.84 | loop fusion | flops 24510464 | bytes 31777792 | tf_op jit(solution)/shard_map/add | solution.py:193
  (299 shorter events, 200.8 us)
Async XLA Ops:
  7.2 5.8 copy-start.56
  7.2 63.0 %copy-start.1 = (bf16[4,704,512]{2,1,0:T(8,128)(2,1)S(1)}, bf16[4,704,512]{2,1,0:T(8,128)(2,1)}, u32[]{:S(2)}) copy-start(bf16[4,704,512]{2,1,0:T(8,128)(2,1)} %param.17) | copy-start | bytes 8650756
  7.2 7.0 copy-start.49
  7.2 7.2 copy-start.50
  7.2 7.5 copy-start.51
  7.2 7.7 copy-start.52
  7.2 8.0 copy-start.53
  7.3 31.8 %copy-start.42 = (bf16[64,3,128]{2,0,1:T(8,128)(2,1)S(1)}, bf16[64,3,128]{2,0,1:T(8,128)(2,1)}, u32[]{:S(2)}) copy-start(bf16[64,3,128]{2,0,1:T(8,128)(2,1)} %param.22) | copy-start | bytes 147460
  7.3 320.3 %all-gather.3.cloned.1.call-start = ((), (), s32[]{:S(2)}) async-start(), calls=%async_computation.6 | async-start | bytes 28835840 | tf_op jit(solution)/shard_map/all_gather | solution.py:146
  12.9 60.3 %copy-start.29 = (f32[2816]{0:T(1024)}, f32[2816]{0:T(1024)S(1)}, u32[]{:S(2)}) copy-start(f32[2816]{0:T(1024)S(1)} %div.49) | copy-start | bytes 33796
  12.9 85.3 %copy-start.47 = (f32[32]{0:T(128)}, f32[32]{0:T(128)S(1)}, u32[]{:S(2)}) copy-start(f32[32]{0:T(128)S(1)} %multiply_exponential_fusion) | copy-start | bytes 388
  38.9 34.3 %copy-start.39 = (f32[512]{0:T(512)}, f32[512]{0:T(512)S(1)}, u32[]{:S(2)}) copy-start(f32[512]{0:T(512)S(1)} %convert_element_type.200) | copy-start | bytes 6148
  39.0 34.2 %copy-start.36 = (f32[2816]{0:T(1024)}, f32[2816]{0:T(1024)S(1)}, u32[]{:S(2)}) copy-start(f32[2816]{0:T(1024)S(1)} %add.108) | copy-start | bytes 33796
  39.0 31.1 %copy-start.33 = (f32[2816]{0:T(1024)}, f32[2816]{0:T(1024)S(1)}, u32[]{:S(2)}) copy-start(f32[2816]{0:T(1024)S(1)} %rsqrt.20) | copy-start | bytes 33796
  81.8 16.4 %copy-start.44 = (s32[4,704]{1,0:T(4,128)S(1)}, s32[4,704]{1,0:T(4,128)}, u32[]{:S(2)}) copy-start(s32[4,704]{1,0:T(4,128)} %param.18) | copy-start | bytes 33796
  104.0 10.8 %copy-start.54 = (s32[4]{0:T(128)S(1)}, s32[4]{0:T(128)}, u32[]{:S(2)}) copy-start(s32[4]{0:T(128)} %param.19) | copy-start | bytes 52
  114.8 37.0 %copy-start.43 = (bf16[16,512]{1,0:T(8,128)(2,1)S(1)}, bf16[16,512]{1,0:T(8,128)(2,1)}, u32[]{:S(2)}) copy-start(bf16[16,512]{1,0:T(8,128)(2,1)} %param.23) | copy-start | bytes 49156
  186.9 307.1 %all-reduce.14.cloned.1.call-start = ((), (), s32[]{:S(2)}) async-start(), calls=%async_computation.5 | async-start | bytes 11534336 | tf_op jit(solution)/shard_map/psum | solution.py:163
  356.6 20.4 %copy-start.9 = (bf16[2816,512]{1,0:T(8,128)(2,1)}, bf16[2816,512]{1,0:T(8,128)(2,1)S(1)}, u32[]{:S(2)}) copy-start(bf16[2816,512]{1,0:T(8,128)(2,1)S(1)} %add_convert_fusion.2) | copy-start | bytes 8650756
  358.3 18.7 %copy-start.7 = (f32[2816,512]{1,0:T(8,128)}, f32[2816,512]{1,0:T(8,128)S(1)}, u32[]{:S(2)}) copy-start(f32[2816,512]{1,0:T(8,128)S(1)} %fusion.97) | copy-start | bytes 17301508
  387.5 6.9 copy-start.28
  394.4 4.8 copy-start.16
  399.2 94.8 %copy-start.32 = (f32[2816]{0:T(1024)S(1)}, f32[2816]{0:T(1024)}, u32[]{:S(2)}) copy-start(f32[2816]{0:T(1024)} %copy-done.31) | copy-start | bytes 33796
  401.7 98.7 %copy-start.38 = (f32[2816]{0:T(1024)S(1)}, f32[2816]{0:T(1024)}, u32[]{:S(2)}) copy-start(f32[2816]{0:T(1024)} %add.116) | copy-start | bytes 33796
  494.1 6.4 copy-start.8
  500.5 5.0 copy-start.14
  507.9 10.3 %copy-start.5 = (bf16[2816,512]{1,0:T(8,128)(2,1)}, bf16[2816,512]{1,0:T(8,128)(2,1)S(1)}, u32[]{:S(2)}) copy-start(bf16[2816,512]{1,0:T(8,128)(2,1)S(1)} %fusion.70) | copy-start | bytes 8650756
  507.9 10.3 %copy-start.55 = (s32[4]{0:T(128)S(1)}, s32[4]{0:T(128)}, u32[]{:S(2)}) copy-start(s32[4]{0:T(128)} %param.19) | copy-start | bytes 52
  520.2 5.8 copy-start
  552.8 5.8 copy-start
  585.4 5.8 copy-start
  618.0 5.8 copy-start
  659.6 15.7 %copy-start.24 = (bf16[512,3,128]{2,0,1:T(8,128)(2,1)S(1)}, bf16[512,3,128]{2,0,1:T(8,128)(2,1)}, u32[]{:S(2)}) copy-start(bf16[512,3,128]{2,0,1:T(8,128)(2,1)} %copy-done.23) | copy-start | bytes 1179652
  661.1 14.2 %copy-start.25 = (bf16[2816,1,128]{2,0,1:T(8,128)(2,1)}, bf16[2816,1,128]{2,0,1:T(8,128)(2,1)S(1)}, u32[]{:S(2)}) copy-start(bf16[2816,1,128]{2,0,1:T(8,128)(2,1)S(1)} %copy.101) | copy-start | bytes 2162692
  669.5 14.5 %all-to-all-start.3 = ((bf16[8,1,64]{2,1,0:T(2,128)(2,1)}), bf16[8,1,64]{2,1,0:T(2,128)(2,1)S(1)}, u32[]{:S(2)}, u32[]{:S(2)}) async-start(bf16[8,1,64]{2,1,0:T(2,128)(2,1)} %convert_element_type.242), calls=%async_computation.3 | async-start | bytes 8192 | tf_op jit(solution)/shard_map/all_to_all | solution.py:20
  675.0 117.0 %all-reduce.16.cloned.1.call-start = ((), (), s32[]{:S(2)}) async-start(), calls=%async_computation.7 | async-start | bytes 11534336 | tf_op jit(solution)/shard_map/psum | solution.py:154
  684.0 13.9 %copy-start.26 = (bf16[512,512]{1,0:T(8,128)(2,1)S(1)}, bf16[512,512]{1,0:T(8,128)(2,1)}, u32[]{:S(2)}) copy-start(bf16[512,512]{1,0:T(8,128)(2,1)} %convolution_convert_fusion.3) | copy-start | bytes 1572868
  684.0 17.4 %all-to-all-start.2 = ((bf16[8,16,512]{2,1,0:T(8,128)(2,1)}), bf16[8,16,512]{2,1,0:T(8,128)(2,1)}, u32[]{:S(2)}, u32[]{:S(2)}) async-start(bf16[8,16,512]{2,1,0:T(8,128)(2,1)} %bitcast.33), calls=%async_computation.2 | async-start | bytes 262144 | tf_op jit(solution)/shard_map/all_to_all | solution.py:20
  690.1 17.3 %copy-start.12 = (bf16[2816,512]{1,0:T(8,128)(2,1)S(1)}, bf16[2816,512]{1,0:T(8,128)(2,1)}, u32[]{:S(2)}) copy-start(bf16[2816,512]{1,0:T(8,128)(2,1)} %copy-done.11) | copy-start | bytes 8650756
  701.5 33.6 %all-to-all-start.4 = ((bf16[8,64,1026]{2,1,0:T(8,128)(2,1)}), bf16[8,64,1026]{2,1,0:T(8,128)(2,1)}, u32[]{:S(2)}, u32[]{:S(2)}) async-start(bf16[8,64,1026]{2,1,0:T(8,128)(2,1)} %concatenate.60), calls=%async_computation.4 | async-start | bytes 2359296 | tf_op jit(solution)/shard_map/all_to_all | solution.py:20
  707.5 84.5 %copy-start.30 = (f32[2816]{0:T(1024)S(1)}, f32[2816]{0:T(1024)}, u32[]{:S(2)}) copy-start(f32[2816]{0:T(1024)} %copy-done.29) | copy-start | bytes 33796
  707.5 84.5 %copy-start.40 = (f32[512]{0:T(512)S(1)}, f32[512]{0:T(512)}, u32[]{:S(2)}) copy-start(f32[512]{0:T(512)} %copy-done.39) | copy-start | bytes 6148
  710.7 81.3 %copy-start.2 = (bf16[4,704,512]{2,1,0:T(8,128)(2,1)S(1)}, bf16[4,704,512]{2,1,0:T(8,128)(2,1)}, u32[]{:S(2)}) copy-start(bf16[4,704,512]{2,1,0:T(8,128)(2,1)} %param.17) | copy-start | bytes 8650756
  711.1 86.9 %copy-start.37 = (f32[2816]{0:T(1024)S(1)}, f32[2816]{0:T(1024)}, u32[]{:S(2)}) copy-start(f32[2816]{0:T(1024)} %copy-done.36) | copy-start | bytes 33796
  712.2 85.8 %copy-start.34 = (f32[2816]{0:T(1024)S(1)}, f32[2816]{0:T(1024)}, u32[]{:S(2)}) copy-start(f32[2816]{0:T(1024)} %copy-done.33) | copy-start | bytes 33796
  795.4 13.6 %copy-start.22 = (bf16[8,64,384]{2,1,0:T(8,128)(2,1)S(1)}, bf16[8,64,384]{2,1,0:T(8,128)(2,1)}, u32[]{:S(2)}) copy-start(bf16[8,64,384]{2,1,0:T(8,128)(2,1)} %concatenate.55) | copy-start | bytes 1179652
  803.5 11.9 %all-to-all-start = ((bf16[8,1,64]{2,1,0:T(2,128)(2,1)}), bf16[8,1,64]{2,1,0:T(2,128)(2,1)S(1)}, u32[]{:S(2)}, u32[]{:S(2)}) async-start(bf16[8,1,64]{2,1,0:T(2,128)(2,1)} %convert_element_type.240), calls=%async_computation | async-start | bytes 8192 | tf_op jit(solution)/shard_map/all_to_all | solution.py:20
  815.4 16.5 %all-to-all-start.1 = ((bf16[8,64,385]{2,1,0:T(8,128)(2,1)}), bf16[8,64,385]{2,1,0:T(8,128)(2,1)S(1)}, u32[]{:S(2)}, u32[]{:S(2)}) async-start(bf16[8,64,385]{2,1,0:T(8,128)(2,1)} %pad_maximum_fusion.5), calls=%async_computation.1 | async-start | bytes 1048576 | tf_op jit(solution)/shard_map/all_to_all | solution.py:20
  (20 other events, 48.2 us)
Sparse Core Ops, SparseCore 0:
  187.0 140.4 all-gather.2
  382.9 111.0 all-reduce.13
  680.1 111.8 all-reduce.15
